TPU v7x, 256 devices: a whole 4x4x8 slice. The times are simulated.
256 devices in a mesh: row: 16 (over y, z_lo), col: 16 (over z_hi, x, core).
Axes of the slice: x: 4, y: 4, z: 8 (z_hi: 2, z_lo: 4; z = z_hi * 4 + z_lo), core: 2. Of those that a mesh axis runs over, the one named last changes fastest.
Arguments:
- start_vectors: float32 [64, 32768], P(None, ('row', 'col')), may hold values from -6 to 6
- cluster_order: int32 [256, 128], P(('row', 'col')), may hold values from 0 to 127, each once within a row
- weights: bfloat16 [32768, 16, 2048], P('row', 'col'), may hold values from 0 to 1, as said below
- block_mask: int32 [256, 16, 16], P('row', 'col'), may hold values 0 or 1
Outputs:
- embedding: float32 [64, 32768], P(None, ('row', 'col'))
Inputs may be any that keep to these rules, and one draw needn't show every extreme that they name: Each row of cluster_order holds every number of 0 to 127 once. `block_mask`: entries below the diagonal blocks are read only through their mirror. `weights`: every node except the last of its cluster block has a positive weight to the next node of its cluster block.
All inputs are finite; a program needn't handle non-finite values.
Results may differ from a plain program's by a relative error of at most 0.00087.
Values may be sent and summed in bfloat16 or wider, within the bound.
A program may use at most 64 MiB of HBM per device.

v0:
```python
import math
import jax
import jax.numpy as jnp
from jax import lax
from jax.sharding import PartitionSpec as P

ITERS = 3


def orthonormalize(panel_in):
    partial_gram = lax.dot_general(
        panel_in,
        panel_in,
        (((1,), (1,)), ((), ())),
        precision=lax.Precision.HIGHEST,
        preferred_element_type=jnp.float32,
    )
    total_gram = lax.psum(partial_gram, ("row", "col"))
    factor = jnp.linalg.cholesky(total_gram)
    return jax.scipy.linalg.solve_triangular(factor, panel_in, lower=True)


def collect_direct(term):
    return lax.psum_scatter(term, "col", scatter_dimension=1, tiled=True)


def direct_part(matrix, vectors):
    return lax.dot_general(
        lax.all_gather(vectors, "row", axis=1, tiled=True),
        matrix,
        (((1,), (1,)), ((), ())),
        preferred_element_type=jnp.float32,
    )


def local(start_vectors, cluster_order, weights, block_mask):
    row_index = lax.axis_index("row")
    col_index = lax.axis_index("col")
    row_count = lax.axis_size("row")
    col_count = lax.axis_size("col")
    block_len = start_vectors.shape[1]
    stored = weights[:, 0, :]
    live_mask = block_mask[:, 0, :]
    local_rows = row_index * col_count * block_len + jnp.arange(
        col_count * block_len, dtype=jnp.int32
    )
    col_position = jnp.arange(row_count * block_len, dtype=jnp.int32)
    local_cols = (
        col_position // block_len * col_count + col_index
    ) * block_len + col_position % block_len
    row_spans = row_index * col_count + jnp.arange(col_count, dtype=jnp.int32)
    col_spans = jnp.arange(row_count, dtype=jnp.int32) * col_count + col_index
    same_block = row_spans[:, None] == col_spans[None, :]
    keep_upper = ((live_mask > 0) | same_block)[:, None, :, None] & (
        local_rows.reshape(col_count, block_len, 1, 1)
        < local_cols.reshape(1, 1, row_count, block_len)
    )
    zero_value = jnp.zeros((), jnp.bfloat16)
    upper_part = jnp.where(
        keep_upper, stored.reshape(col_count, block_len, row_count, block_len), zero_value
    )
    ones_cols = jnp.ones((row_count * block_len,), jnp.bfloat16)
    matrix = upper_part.reshape(col_count * block_len, row_count * block_len)
    ones_rows = jnp.ones((col_count * block_len,), jnp.bfloat16)

    def mirror_sums(term):
        return lax.psum_scatter(term, "row", scatter_dimension=1, tiled=True)

    row_totals = jnp.dot(matrix, ones_cols, preferred_element_type=jnp.float32)[None, :]
    col_totals = jnp.dot(ones_rows, matrix, preferred_element_type=jnp.float32)[None, :]
    degree = collect_direct(row_totals) + mirror_sums(col_totals)
    inverse_root = 1.0 / jnp.sqrt(degree)
    picked = jnp.take_along_axis(
        start_vectors, jnp.broadcast_to(cluster_order, start_vectors.shape), axis=1
    )
    panel_now = orthonormalize(picked)
    for round_index in range(ITERS):
        vectors = (inverse_root * panel_now).astype(jnp.bfloat16)
        panel_now = orthonormalize(
            panel_now
            + inverse_root
            * (
                collect_direct(direct_part(matrix, vectors))
                + mirror_sums(
                    jnp.dot(
                        lax.all_gather(vectors, "col", axis=1, tiled=True),
                        matrix,
                        preferred_element_type=jnp.float32,
                    )
                )
            )
        )
    total_nodes = block_len * row_count * col_count
    return math.sqrt(total_nodes) * panel_now


def solution(mesh):
    placed = (
        P(None, ("row", "col")),
        P(("row", "col"), None),
        P("row", "col", None),
        P("row", "col", None),
    )
    return jax.shard_map(
        local, mesh=mesh, in_specs=placed, out_specs=P(None, ("row", "col")), check_vma=False
    )
```

profile of v0, /device:TPU:1, one launch (start us, length us, event | category | flops | bytes accessed | tf_op | source)
XLA Modules:
  0.0 1080.2 jit_solution(14854760492870772984)
XLA Ops:
  6.5 0.7 broadcast_compare_fusion
  7.3 0.1 bitcast_or_fusion
  7.4 1.1 and.66
  8.5 7.7 fusion
  16.3 3.2 copy-done.1
  19.5 3.4 convolution_bitcast_fusion.1
  23.0 7.7 convolution_bitcast_fusion
  30.9 50.7 %gather_fusion = f32[8192]{0:T(1024)S(1)} fusion(f32[64,128]{1,0:T(8,128)S(1)} %copy-done, s32[8192]{0:T(1024)S(1)} %or_bitcast_fusion), kind=kCustom, calls=%fused_computation | custom fusion | bytes 131072 | tf_op jit(solution)/shard_map/jit(take_along_axis)/gather | solution.py:73
  81.5 0.2 fusion.16
  81.7 82.8 %psum.28 = f32[64,64]{0,1:T(8,128)S(1)} all-reduce(f32[64,64]{0,1:T(8,128)S(1)} %fusion.16), channel_id=1, replica_groups=mesh['row'=16,'col'=16] {'row','col'}, use_global_device_ids=true, to_apply=%region_0.1 | all-reduce | flops 4096 | bytes 32768 | tf_op jit(solution)/shard_map/psum | solution.py:18
  164.6 0.1 copy.22
  164.7 5.8 cholesky.74
  170.5 0.6 compare_reduce_fusion.3
  171.2 0.7 fusion.1
  171.8 4.9 custom-call.10
  176.8 0.9 copy.34
  177.7 4.9 reduce-scatter.27.cloned.1.call-done
  182.5 0.9 copy.36
  183.4 0.3 multiply_convert_fusion.2
  183.7 32.5 %all_gather.18 = bf16[64,2048]{1,0:T(8,128)(2,1)S(1)} all-gather(bf16[64,128]{1,0:T(8,128)(2,1)S(1)} %get-tuple-element.6), channel_id=1, replica_groups=mesh['row'=16,'col'=16] {'row'}, dimensions={1}, use_global_device_ids=true | all-gather | bytes 278528 | tf_op jit(solution)/shard_map/all_gather | solution.py:29
  216.2 6.9 fusion.59
  223.1 50.3 %all_gather.19 = bf16[64,2048]{1,0:T(8,128)(2,1)S(1)} all-gather(bf16[64,128]{1,0:T(8,128)(2,1)S(1)} %get-tuple-element.6), channel_id=1, replica_groups=mesh['row'=16,'col'=16] {'col'}, dimensions={1}, use_global_device_ids=true | all-gather | bytes 278528 | tf_op jit(solution)/shard_map/all_gather | solution.py:86
  273.5 5.8 fusion.60
  279.4 35.2 %reduce-scatter.13.cloned.1.call-done = f32[64,128]{1,0:T(8,128)} async-done(((f32[64,2048]{1,0:T(8,128)}), f32[64,128]{1,0:T(8,128)}) %reduce-scatter.13.cloned.1.call-update) | async-done | bytes 32784 | tf_op jit(solution)/shard_map/reduce_scatter | solution.py:24
  314.6 75.0 %reduce-scatter.15.cloned.1.call-done = f32[64,128]{1,0:T(8,128)} async-done(((f32[64,2048]{1,0:T(8,128)}), f32[64,128]{1,0:T(8,128)}) %reduce-scatter.15.cloned.1.call-update) | async-done | bytes 32784 | tf_op jit(solution)/shard_map/reduce_scatter | solution.py:67
  389.6 0.8 multiply_add_fusion.2
  390.4 0.2 fusion.61
  390.6 85.2 %psum.29 = f32[64,64]{0,1:T(8,128)S(1)} all-reduce(f32[64,64]{0,1:T(8,128)S(1)} %fusion.61), channel_id=1, replica_groups=mesh['row'=16,'col'=16] {'row','col'}, use_global_device_ids=true, to_apply=%region_7.10 | all-reduce | flops 4096 | bytes 32768 | tf_op jit(solution)/shard_map/psum | solution.py:18
  475.7 0.1 copy.24
  475.8 5.8 cholesky.85
  481.7 0.6 compare_reduce_fusion.2
  482.3 0.7 fusion.2
  483.0 4.9 custom-call.11
  487.9 0.3 multiply_convert_fusion.1
  488.2 34.1 %all_gather.20 = bf16[64,2048]{1,0:T(8,128)(2,1)S(1)} all-gather(bf16[64,128]{1,0:T(8,128)(2,1)S(1)} %get-tuple-element.9), channel_id=1, replica_groups=mesh['row'=16,'col'=16] {'row'}, dimensions={1}, use_global_device_ids=true | all-gather | bytes 278528 | tf_op jit(solution)/shard_map/all_gather | solution.py:29
  522.3 6.9 fusion.62
  529.2 36.1 %all_gather.21 = bf16[64,2048]{1,0:T(8,128)(2,1)S(1)} all-gather(bf16[64,128]{1,0:T(8,128)(2,1)S(1)} %get-tuple-element.9), channel_id=1, replica_groups=mesh['row'=16,'col'=16] {'col'}, dimensions={1}, use_global_device_ids=true | all-gather | bytes 278528 | tf_op jit(solution)/shard_map/all_gather | solution.py:86
  565.3 5.8 fusion.63
  571.2 35.5 %reduce-scatter.17.cloned.1.call-done = f32[64,128]{1,0:T(8,128)} async-done(((f32[64,2048]{1,0:T(8,128)}), f32[64,128]{1,0:T(8,128)}) %reduce-scatter.17.cloned.1.call-update) | async-done | bytes 32784 | tf_op jit(solution)/shard_map/reduce_scatter | solution.py:24
  606.7 74.7 %reduce-scatter.19.cloned.1.call-done = f32[64,128]{1,0:T(8,128)} async-done(((f32[64,2048]{1,0:T(8,128)}), f32[64,128]{1,0:T(8,128)}) %reduce-scatter.19.cloned.1.call-update) | async-done | bytes 32784 | tf_op jit(solution)/shard_map/reduce_scatter | solution.py:67
  681.4 0.8 multiply_add_fusion.1
  682.2 0.2 fusion.64
  682.4 85.6 %psum.30 = f32[64,64]{0,1:T(8,128)S(1)} all-reduce(f32[64,64]{0,1:T(8,128)S(1)} %fusion.64), channel_id=1, replica_groups=mesh['row'=16,'col'=16] {'row','col'}, use_global_device_ids=true, to_apply=%region_10.13 | all-reduce | flops 4096 | bytes 32768 | tf_op jit(solution)/shard_map/psum | solution.py:18
  768.0 0.1 copy.26
  768.1 5.8 cholesky.96
  774.0 0.6 compare_reduce_fusion.1
  774.6 0.7 fusion.3
  775.3 4.9 custom-call.12
  780.2 0.3 multiply_convert_fusion
  780.4 34.1 %all_gather.22 = bf16[64,2048]{1,0:T(8,128)(2,1)S(1)} all-gather(bf16[64,128]{1,0:T(8,128)(2,1)S(1)} %get-tuple-element.11), channel_id=1, replica_groups=mesh['row'=16,'col'=16] {'row'}, dimensions={1}, use_global_device_ids=true | all-gather | bytes 278528 | tf_op jit(solution)/shard_map/all_gather | solution.py:29
  814.5 6.9 fusion.65
  821.5 35.9 %all_gather.23 = bf16[64,2048]{1,0:T(8,128)(2,1)S(1)} all-gather(bf16[64,128]{1,0:T(8,128)(2,1)S(1)} %get-tuple-element.11), channel_id=1, replica_groups=mesh['row'=16,'col'=16] {'col'}, dimensions={1}, use_global_device_ids=true | all-gather | bytes 278528 | tf_op jit(solution)/shard_map/all_gather | solution.py:86
  857.4 5.8 fusion.66
  863.2 35.7 %reduce-scatter.21.cloned.1.call-done = f32[64,128]{1,0:T(8,128)} async-done(((f32[64,2048]{1,0:T(8,128)}), f32[64,128]{1,0:T(8,128)}) %reduce-scatter.21.cloned.1.call-update) | async-done | bytes 32784 | tf_op jit(solution)/shard_map/reduce_scatter | solution.py:24
  899.0 75.8 %reduce-scatter.23.cloned.1.call-done = f32[64,128]{1,0:T(8,128)} async-done(((f32[64,2048]{1,0:T(8,128)}), f32[64,128]{1,0:T(8,128)}) %reduce-scatter.23.cloned.1.call-update) | async-done | bytes 32784 | tf_op jit(solution)/shard_map/reduce_scatter | solution.py:67
  974.7 0.8 multiply_add_fusion
  975.5 0.2 fusion.67
  975.7 84.6 %psum.31 = f32[64,64]{0,1:T(8,128)S(1)} all-reduce(f32[64,64]{0,1:T(8,128)S(1)} %fusion.67), channel_id=1, replica_groups=mesh['row'=16,'col'=16] {'row','col'}, use_global_device_ids=true, to_apply=%region_13.16 | all-reduce | flops 4096 | bytes 32768 | tf_op jit(solution)/shard_map/psum | solution.py:18
  1060.3 0.1 copy.28
  1060.4 5.8 cholesky.107
  1066.3 0.6 compare_reduce_fusion
  1066.9 0.7 fusion.4
  1067.6 4.9 custom-call.13
  1072.5 0.9 convolution_multiply_fusion
  (36 shorter events, 0.7 us)
Async XLA Ops:
  6.5 24.3 %copy-start = (f32[64,128]{1,0:T(8,128)S(1)}, f32[64,128]{1,0:T(8,128)}, u32[]{:S(2)}) copy-start(f32[64,128]{1,0:T(8,128)} %param.7) | copy-start | bytes 98308
  6.5 170.2 %reduce-scatter.25.cloned.1.call-start = ((), (), s32[]{:S(2)}) async-start(), calls=%async_computation.14 | async-start | bytes 1114112
  16.3 3.2 copy-start.1
  22.9 7.9 copy-start.2
  22.9 159.6 %reduce-scatter.27.cloned.1.call-start = ((), (), s32[]{:S(2)}) async-start(), calls=%async_computation.15 | async-start | bytes 1114112
  30.7 283.8 %reduce-scatter.13.cloned.1.call-start = ((), (), s32[]{:S(2)}) async-start(), calls=%async_computation.8 | async-start | bytes 557056 | tf_op jit(solution)/shard_map/reduce_scatter | solution.py:24
  223.1 166.5 %reduce-scatter.15.cloned.1.call-start = ((), (), s32[]{:S(2)}) async-start(), calls=%async_computation.9 | async-start | bytes 557056 | tf_op jit(solution)/shard_map/reduce_scatter | solution.py:67
  279.3 327.4 %reduce-scatter.17.cloned.1.call-start = ((), (), s32[]{:S(2)}) async-start(), calls=%async_computation.10 | async-start | bytes 557056 | tf_op jit(solution)/shard_map/reduce_scatter | solution.py:24
  529.2 152.2 %reduce-scatter.19.cloned.1.call-start = ((), (), s32[]{:S(2)}) async-start(), calls=%async_computation.11 | async-start | bytes 557056 | tf_op jit(solution)/shard_map/reduce_scatter | solution.py:67
  571.1 327.8 %reduce-scatter.21.cloned.1.call-start = ((), (), s32[]{:S(2)}) async-start(), calls=%async_computation.12 | async-start | bytes 557056 | tf_op jit(solution)/shard_map/reduce_scatter | solution.py:24
  821.4 153.3 %reduce-scatter.23.cloned.1.call-start = ((), (), s32[]{:S(2)}) async-start(), calls=%async_computation.13 | async-start | bytes 557056 | tf_op jit(solution)/shard_map/reduce_scatter | solution.py:67
Sparse Core Ops, SparseCore 0:
  23.1 81.6 reduce-scatter.24
  107.3 75.2 reduce-scatter.26
  223.2 91.2 reduce-scatter.12
  316.9 72.6 reduce-scatter.14
  529.3 77.3 reduce-scatter.16
  609.1 72.2 reduce-scatter.18
  821.5 77.3 reduce-scatter.20
  901.4 73.2 reduce-scatter.22
where the time goes:
time: 1080 us
  blocking collectives  561 us (52%)
  waiting for transfers between devices  337 us (31%)
  other arithmetic  59.2 us (5%)
  local copies, waits for them, and re-layouts  57.1 us (5%)
  matrix products  51.7 us (5%)
  between operations  13.8 us (1%)
    psum x4, blocking collectives, orthonormalize(): total_gram = lax.psum(partial_gram, ('row', 'col'))  338 us
    reduce_scatter x3, waiting for transfers between devices, mirror_sums(): return lax.psum_scatter(term, 'row', scatter_dimension=1, tiled=True)  225 us
    all_gather x3, blocking collectives, local(): lax.all_gather(vectors, 'col', axis=1, tiled=True)  122 us
    reduce_scatter x3, waiting for transfers between devices, collect_direct(): return lax.psum_scatter(term, 'col', scatter_dimension=1, tiled=True)  106 us
    all_gather x3, blocking collectives, direct_part(): lax.all_gather(vectors, 'row', axis=1, tiled=True)  101 us
    gather x1, local copies, waits for them, and re-layouts, local(): jnp.take_along_axis(start_vectors, jnp.broadcast_to(cluster_order, start_...  50.7 us
    another operation x12, other arithmetic, orthonormalize(): factor = jnp.linalg.cholesky(total_gram)  26.1 us
    another operation x8, other arithmetic, orthonormalize(): return jax.scipy.linalg.solve_triangular(factor, panel_in, lower=True)  22.2 us
  transfers between devices with their start and end apart: 8, of which 7 were waited for; matrix products, arithmetic and copies ran while one was open for 8% of the time, Pallas kernels for 0%

commit v1 on v0

--- a/solution.py
+++ b/solution.py
@@ -15,7 +15,9 @@
         precision=lax.Precision.HIGHEST,
         preferred_element_type=jnp.float32,
     )
-    total_gram = lax.psum(partial_gram, ("row", "col"))
+    total_gram = partial_gram
+    for mesh_axis in ("row", "col"):
+        total_gram = lax.psum(total_gram, mesh_axis)
     factor = jnp.linalg.cholesky(total_gram)
     return jax.scipy.linalg.solve_triangular(factor, panel_in, lower=True)
 

time: 1080 us -> 1400 us (1.30)
  blocking collectives: 561 us -> 862 us
    psum x4 -> x8, blocking collectives: 338 us -> 647 us  [orthonormalize(): total_gram = lax.psum(total_gram, mesh_axis)]
    reduce_scatter x3, waiting for transfers between devices: 106 us -> 121 us  [collect_direct(): return lax.psum_scatter(term, 'col', scatter_dimension=1, tiled=True)]
  transfers between devices with their start and end apart: 8 -> 8, of which waited for: 7 -> 6; matrix products, arithmetic and copies ran while one was open for 8% -> 6% of each run, Pallas kernels for 0% -> 0%
where the time goes in v1:
time: 1400 us; the launch traced here: 1390 us
  blocking collectives  862 us (62%)
  waiting for transfers between devices  348 us (25%)
  other arithmetic  59.2 us (4%)
  local copies, waits for them, and re-layouts  57.2 us (4%)
  matrix products  51.7 us (4%)
    psum x8, blocking collectives, orthonormalize(): total_gram = lax.psum(total_gram, mesh_axis)  647 us
    reduce_scatter x3, waiting for transfers between devices, mirror_sums(): return lax.psum_scatter(term, 'row', scatter_dimension=1, tiled=True)  226 us
    reduce_scatter x3, waiting for transfers between devices, collect_direct(): return lax.psum_scatter(term, 'col', scatter_dimension=1, tiled=True)  121 us
    all_gather x3, blocking collectives, local(): lax.all_gather(vectors, 'col', axis=1, tiled=True)  119 us
    all_gather x3, blocking collectives, direct_part(): lax.all_gather(vectors, 'row', axis=1, tiled=True)  96.5 us
    gather x1, local copies, waits for them, and re-layouts, local(): jnp.take_along_axis(start_vectors, jnp.broadcast_to(cluster_order, start_...  50.7 us
  transfers between devices with their start and end apart: 8, of which 6 were waited for; matrix products, arithmetic and copies ran while one was open for 6% of the time, Pallas kernels for 0%

profile of v1, /device:TPU:1, one launch (start us, length us, event | category | flops | bytes accessed | tf_op | source)
XLA Modules:
  0.0 1392.0 jit_solution(7141730405209336479)
XLA Ops:
  6.5 0.7 broadcast_compare_fusion
  7.3 0.1 bitcast_or_fusion
  7.4 1.1 and.66
  8.5 7.7 fusion
  16.3 3.2 copy-done.1
  19.5 3.4 convolution_bitcast_fusion.1
  23.0 7.7 convolution_bitcast_fusion
  30.9 50.7 %gather_fusion = f32[8192]{0:T(1024)S(1)} fusion(f32[64,128]{1,0:T(8,128)S(1)} %copy-done, s32[8192]{0:T(1024)S(1)} %or_bitcast_fusion), kind=kCustom, calls=%fused_computation | custom fusion | bytes 131072 | tf_op jit(solution)/shard_map/jit(take_along_axis)/gather | solution.py:75
  81.5 0.2 fusion.16
  81.7 69.3 %psum.56 = f32[64,64]{0,1:T(8,128)S(1)} all-reduce(f32[64,64]{0,1:T(8,128)S(1)} %fusion.16), channel_id=1, replica_groups=mesh['row'=16,'col'=16] {'row'}, use_global_device_ids=true, to_apply=%region_0.1 | all-reduce | flops 4096 | bytes 32768 | tf_op jit(solution)/shard_map/psum | solution.py:20
  151.0 89.9 %psum.57 = f32[64,64]{0,1:T(8,128)S(1)} all-reduce(f32[64,64]{0,1:T(8,128)S(1)} %psum.56), channel_id=1, replica_groups=mesh['row'=16,'col'=16] {'col'}, use_global_device_ids=true, to_apply=%region_1.2 | all-reduce | flops 4096 | bytes 32768 | tf_op jit(solution)/shard_map/psum | solution.py:20
  241.0 0.1 copy.22
  241.1 5.8 cholesky.74
  246.9 0.6 compare_reduce_fusion.3
  247.6 0.7 fusion.1
  248.2 4.9 custom-call.10
  253.2 0.9 copy.34
  254.1 0.9 copy.36
  255.0 0.3 multiply_convert_fusion.2
  255.3 32.1 %all_gather.18 = bf16[64,2048]{1,0:T(8,128)(2,1)S(1)} all-gather(bf16[64,128]{1,0:T(8,128)(2,1)S(1)} %get-tuple-element.6), channel_id=1, replica_groups=mesh['row'=16,'col'=16] {'row'}, dimensions={1}, use_global_device_ids=true | all-gather | bytes 278528 | tf_op jit(solution)/shard_map/all_gather | solution.py:31
  287.4 6.9 fusion.59
  294.4 39.5 %all_gather.19 = bf16[64,2048]{1,0:T(8,128)(2,1)S(1)} all-gather(bf16[64,128]{1,0:T(8,128)(2,1)S(1)} %get-tuple-element.6), channel_id=1, replica_groups=mesh['row'=16,'col'=16] {'col'}, dimensions={1}, use_global_device_ids=true | all-gather | bytes 278528 | tf_op jit(solution)/shard_map/all_gather | solution.py:88
  333.9 5.8 fusion.60
  339.8 39.8 %reduce-scatter.13.cloned.1.call-done = f32[64,128]{1,0:T(8,128)} async-done(((f32[64,2048]{1,0:T(8,128)}), f32[64,128]{1,0:T(8,128)}) %reduce-scatter.13.cloned.1.call-update) | async-done | bytes 32784 | tf_op jit(solution)/shard_map/reduce_scatter | solution.py:26
  379.6 75.7 %reduce-scatter.15.cloned.1.call-done = f32[64,128]{1,0:T(8,128)} async-done(((f32[64,2048]{1,0:T(8,128)}), f32[64,128]{1,0:T(8,128)}) %reduce-scatter.15.cloned.1.call-update) | async-done | bytes 32784 | tf_op jit(solution)/shard_map/reduce_scatter | solution.py:69
  455.3 0.8 multiply_add_fusion.2
  456.1 0.2 fusion.61
  456.3 61.4 %psum.58 = f32[64,64]{0,1:T(8,128)S(1)} all-reduce(f32[64,64]{0,1:T(8,128)S(1)} %fusion.61), channel_id=1, replica_groups=mesh['row'=16,'col'=16] {'row'}, use_global_device_ids=true, to_apply=%region_8.11 | all-reduce | flops 4096 | bytes 32768 | tf_op jit(solution)/shard_map/psum | solution.py:20
  517.7 100.9 %psum.59 = f32[64,64]{0,1:T(8,128)S(1)} all-reduce(f32[64,64]{0,1:T(8,128)S(1)} %psum.58), channel_id=1, replica_groups=mesh['row'=16,'col'=16] {'col'}, use_global_device_ids=true, to_apply=%region_9.12 | all-reduce | flops 4096 | bytes 32768 | tf_op jit(solution)/shard_map/psum | solution.py:20
  618.7 5.8 cholesky.85
  624.6 0.6 compare_reduce_fusion.2
  625.2 0.7 fusion.2
  625.9 4.9 custom-call.11
  630.8 0.3 multiply_convert_fusion.1
  631.0 32.1 %all_gather.20 = bf16[64,2048]{1,0:T(8,128)(2,1)S(1)} all-gather(bf16[64,128]{1,0:T(8,128)(2,1)S(1)} %get-tuple-element.9), channel_id=1, replica_groups=mesh['row'=16,'col'=16] {'row'}, dimensions={1}, use_global_device_ids=true | all-gather | bytes 278528 | tf_op jit(solution)/shard_map/all_gather | solution.py:31
  663.1 6.9 fusion.62
  670.0 39.5 %all_gather.21 = bf16[64,2048]{1,0:T(8,128)(2,1)S(1)} all-gather(bf16[64,128]{1,0:T(8,128)(2,1)S(1)} %get-tuple-element.9), channel_id=1, replica_groups=mesh['row'=16,'col'=16] {'col'}, dimensions={1}, use_global_device_ids=true | all-gather | bytes 278528 | tf_op jit(solution)/shard_map/all_gather | solution.py:88
  709.5 5.8 fusion.63
  715.5 40.6 %reduce-scatter.17.cloned.1.call-done = f32[64,128]{1,0:T(8,128)} async-done(((f32[64,2048]{1,0:T(8,128)}), f32[64,128]{1,0:T(8,128)}) %reduce-scatter.17.cloned.1.call-update) | async-done | bytes 32784 | tf_op jit(solution)/shard_map/reduce_scatter | solution.py:26
  756.1 75.0 %reduce-scatter.19.cloned.1.call-done = f32[64,128]{1,0:T(8,128)} async-done(((f32[64,2048]{1,0:T(8,128)}), f32[64,128]{1,0:T(8,128)}) %reduce-scatter.19.cloned.1.call-update) | async-done | bytes 32784 | tf_op jit(solution)/shard_map/reduce_scatter | solution.py:69
  831.1 0.8 multiply_add_fusion.1
  831.8 0.2 fusion.64
  832.0 61.6 %psum.60 = f32[64,64]{0,1:T(8,128)S(1)} all-reduce(f32[64,64]{0,1:T(8,128)S(1)} %fusion.64), channel_id=1, replica_groups=mesh['row'=16,'col'=16] {'row'}, use_global_device_ids=true, to_apply=%region_12.15 | all-reduce | flops 4096 | bytes 32768 | tf_op jit(solution)/shard_map/psum | solution.py:20
  893.6 101.3 %psum.61 = f32[64,64]{0,1:T(8,128)S(1)} all-reduce(f32[64,64]{0,1:T(8,128)S(1)} %psum.60), channel_id=1, replica_groups=mesh['row'=16,'col'=16] {'col'}, use_global_device_ids=true, to_apply=%region_13.16 | all-reduce | flops 4096 | bytes 32768 | tf_op jit(solution)/shard_map/psum | solution.py:20
  995.0 5.8 cholesky.96
  1000.9 0.6 compare_reduce_fusion.1
  1001.5 0.7 fusion.3
  1002.2 4.9 custom-call.12
  1007.1 0.3 multiply_convert_fusion
  1007.4 32.3 %all_gather.22 = bf16[64,2048]{1,0:T(8,128)(2,1)S(1)} all-gather(bf16[64,128]{1,0:T(8,128)(2,1)S(1)} %get-tuple-element.11), channel_id=1, replica_groups=mesh['row'=16,'col'=16] {'row'}, dimensions={1}, use_global_device_ids=true | all-gather | bytes 278528 | tf_op jit(solution)/shard_map/all_gather | solution.py:31
  1039.6 6.9 fusion.65
  1046.6 39.7 %all_gather.23 = bf16[64,2048]{1,0:T(8,128)(2,1)S(1)} all-gather(bf16[64,128]{1,0:T(8,128)(2,1)S(1)} %get-tuple-element.11), channel_id=1, replica_groups=mesh['row'=16,'col'=16] {'col'}, dimensions={1}, use_global_device_ids=true | all-gather | bytes 278528 | tf_op jit(solution)/shard_map/all_gather | solution.py:88
  1086.3 5.8 fusion.66
  1092.1 40.8 %reduce-scatter.21.cloned.1.call-done = f32[64,128]{1,0:T(8,128)} async-done(((f32[64,2048]{1,0:T(8,128)}), f32[64,128]{1,0:T(8,128)}) %reduce-scatter.21.cloned.1.call-update) | async-done | bytes 32784 | tf_op jit(solution)/shard_map/reduce_scatter | solution.py:26
  1133.0 75.7 %reduce-scatter.23.cloned.1.call-done = f32[64,128]{1,0:T(8,128)} async-done(((f32[64,2048]{1,0:T(8,128)}), f32[64,128]{1,0:T(8,128)}) %reduce-scatter.23.cloned.1.call-update) | async-done | bytes 32784 | tf_op jit(solution)/shard_map/reduce_scatter | solution.py:69
  1208.7 0.8 multiply_add_fusion
  1209.5 0.2 fusion.67
  1209.7 60.9 %psum.62 = f32[64,64]{0,1:T(8,128)S(1)} all-reduce(f32[64,64]{0,1:T(8,128)S(1)} %fusion.67), channel_id=1, replica_groups=mesh['row'=16,'col'=16] {'row'}, use_global_device_ids=true, to_apply=%region_16.19 | all-reduce | flops 4096 | bytes 32768 | tf_op jit(solution)/shard_map/psum | solution.py:20
  1270.6 101.5 %psum.63 = f32[64,64]{0,1:T(8,128)S(1)} all-reduce(f32[64,64]{0,1:T(8,128)S(1)} %psum.62), channel_id=1, replica_groups=mesh['row'=16,'col'=16] {'col'}, use_global_device_ids=true, to_apply=%region_17.20 | all-reduce | flops 4096 | bytes 32768 | tf_op jit(solution)/shard_map/psum | solution.py:20
  1372.2 5.8 cholesky.107
  1378.0 0.6 compare_reduce_fusion
  1378.7 0.7 fusion.4
  1379.3 4.9 custom-call.13
  1384.2 0.9 convolution_multiply_fusion
  (40 shorter events, 0.9 us)
Async XLA Ops:
  6.5 24.3 %copy-start = (f32[64,128]{1,0:T(8,128)S(1)}, f32[64,128]{1,0:T(8,128)}, u32[]{:S(2)}) copy-start(f32[64,128]{1,0:T(8,128)} %param.7) | copy-start | bytes 98308
  6.5 246.6 %reduce-scatter.25.cloned.1.call-start = ((), (), s32[]{:S(2)}) async-start(), calls=%async_computation.14 | async-start | bytes 1114112
  16.3 3.2 copy-start.1
  22.9 7.9 copy-start.2
  22.9 231.1 %reduce-scatter.27.cloned.1.call-start = ((), (), s32[]{:S(2)}) async-start(), calls=%async_computation.15 | async-start | bytes 1114112
  30.7 348.9 %reduce-scatter.13.cloned.1.call-start = ((), (), s32[]{:S(2)}) async-start(), calls=%async_computation.8 | async-start | bytes 557056 | tf_op jit(solution)/shard_map/reduce_scatter | solution.py:26
  294.3 161.0 %reduce-scatter.15.cloned.1.call-start = ((), (), s32[]{:S(2)}) async-start(), calls=%async_computation.9 | async-start | bytes 557056 | tf_op jit(solution)/shard_map/reduce_scatter | solution.py:69
  339.8 416.3 %reduce-scatter.17.cloned.1.call-start = ((), (), s32[]{:S(2)}) async-start(), calls=%async_computation.10 | async-start | bytes 557056 | tf_op jit(solution)/shard_map/reduce_scatter | solution.py:26
  670.0 161.1 %reduce-scatter.19.cloned.1.call-start = ((), (), s32[]{:S(2)}) async-start(), calls=%async_computation.11 | async-start | bytes 557056 | tf_op jit(solution)/shard_map/reduce_scatter | solution.py:69
  715.4 417.6 %reduce-scatter.21.cloned.1.call-start = ((), (), s32[]{:S(2)}) async-start(), calls=%async_computation.12 | async-start | bytes 557056 | tf_op jit(solution)/shard_map/reduce_scatter | solution.py:26
  1046.6 162.1 %reduce-scatter.23.cloned.1.call-start = ((), (), s32[]{:S(2)}) async-start(), calls=%async_computation.13 | async-start | bytes 557056 | tf_op jit(solution)/shard_map/reduce_scatter | solution.py:69
Sparse Core Ops, SparseCore 0:
  23.1 81.7 reduce-scatter.24
  107.3 74.5 reduce-scatter.26
  294.5 85.1 reduce-scatter.12
  382.0 73.2 reduce-scatter.14
  670.1 85.9 reduce-scatter.16
  758.4 72.5 reduce-scatter.18
  1046.7 86.2 reduce-scatter.20
  1135.5 73.1 reduce-scatter.22
